TPU v7x, 32 devices: a whole 2x2x4 slice. The times are simulated.
32 devices in a mesh: tok: 4 (over y, x), col: 8 (over z, core).
Axes of the slice: x: 2, y: 2, z: 4, core: 2. Of those that a mesh axis runs over, the one named last changes fastest.
Arguments:
- activations: bfloat16 [8192, 8192], P('tok', 'col'), may hold values from -60 to 60, as said below
- weight: bfloat16 [8192, 8192], P('tok', 'col'), may hold values from -6 to 6
- keep_mask: int32 [8192, 8192], P('tok', 'col'), may hold values from 0 to 1
Outputs:
- new_weight: bfloat16 [8192, 8192], P('tok', 'col')
Inputs may be any that keep to these rules, and one draw needn't show every extreme that they name: activations of calibration tokens.
All inputs are finite; a program needn't handle non-finite values.
Results may differ from a plain program's by a relative error of at most 0.00115.
Values may be sent and summed in bfloat16 or wider, within the bound.
No kernel may reach another device: no remote copies, remote signals or barrier semaphores. Data moves between devices by JAX's collectives and lax.ppermute only.
A program may use at most 128 MiB of HBM per device.

v0:
```python
import jax
import jax.numpy as jnp
from jax import lax
from jax.sharding import PartitionSpec as P

B = 1024
ITERS = 4


def per_device(activations, weight, keep_mask):
    highest = lax.Precision.HIGHEST
    n_col = lax.axis_size("col")
    n_tok = lax.axis_size("tok")
    tok_rows = activations.shape[0]
    panel_width = B // n_col
    total_count = tok_rows * n_tok
    partial_panel = lax.dot_general(
        activations,
        lax.all_gather(activations[:, :panel_width], "col", axis=1, tiled=True),
        (((0,), (0,)), ((), ())),
        preferred_element_type=jnp.float32,
    )
    block_part = lax.psum(partial_panel[:panel_width], "tok") / total_count
    diagonal_block = lax.all_gather(block_part, "col", axis=0, tiled=True)
    identity = jnp.eye(B, dtype=jnp.float32)
    damping = 0.01 * jnp.mean(jnp.diagonal(diagonal_block))
    damped = diagonal_block + damping * identity
    frobenius = jnp.sqrt(jnp.sum(damped * damped))
    col_index = lax.axis_index("col")
    row_ids = col_index * panel_width + lax.iota(jnp.int32, panel_width)
    iterate = (row_ids[:, None] == lax.iota(jnp.int32, B)[None, :]).astype(jnp.float32) / frobenius
    for sweep in range(ITERS):
        if sweep == 0:
            whole = identity / frobenius
        else:
            whole = lax.all_gather(iterate.astype(jnp.bfloat16), "col", axis=0, tiled=True).astype(
                iterate.dtype
            )
        product = jnp.dot(iterate, damped, precision=highest)
        iterate = 2.0 * iterate - jnp.dot(product, whole, precision=highest)
    inverse = lax.all_gather(iterate, "col", axis=0, tiled=True)
    remainder = lax.psum(partial_panel[panel_width:], "tok") / total_count
    hessian_panel = jnp.concatenate([block_part, remainder], axis=0)
    pruned = jnp.where(
        keep_mask[:, :panel_width] == 0, weight[:, :panel_width], jnp.zeros((), jnp.bfloat16)
    )
    pruned_panel = lax.all_gather(pruned, "col", axis=1, tiled=True).astype(jnp.float32)
    factor_rows = jnp.dot(pruned_panel, inverse, precision=highest)
    correction = lax.dot_general(
        factor_rows, hessian_panel, (((1,), (1,)), ((), ())), precision=highest
    )
    kept = keep_mask.astype(jnp.float32)
    return (kept * (weight.astype(jnp.float32) - correction)).astype(jnp.bfloat16)


def solution(mesh):
    return jax.shard_map(
        per_device,
        mesh=mesh,
        in_specs=(P("tok", "col"), P("tok", "col"), P("tok", "col")),
        out_specs=P("tok", "col"),
        check_vma=False,
    )
```

profile of v0, /device:TPU:0, one launch (start us, length us, event | category | flops | bytes accessed | tf_op | source)
XLA Modules:
  0.0 493.3 jit_solution(1033233946870937970)
XLA Ops:
  6.5 0.0 all-gather.10.cloned.1.call-start
  6.5 1.9 slice.17
  8.4 0.0 all-gather.10.cloned.1.call-update
  8.4 0.0 all-reduce.3.cloned.1.call-start
  8.5 51.0 %all-gather.10.cloned.1.call-done = bf16[2048,1024]{1,0:T(8,128)(2,1)} async-done(((bf16[2048,128]{1,0:T(8,128)(2,1)}), bf16[2048,1024]{1,0:T(8,128)(2,1)}) %all-gather.10.cloned.1.call-update) | async-done | bytes 4194320 | tf_op jit(solution)/shard_map/all_gather | solution.py:19
  59.5 7.6 %fusion.31 = f32[1024,1024]{1,0:T(8,128)S(1)} fusion(bf16[2048,1024]{1,0:T(8,128)(2,1)} %param.3, bf16[2048,1024]{1,0:T(8,128)(2,1)} %all-gather.10.cloned.1.call-done), kind=kOutput, calls=%fused_computation.42 | convolution fusion | flops 4294967296 | bytes 12582912 | tf_op jit(solution)/shard_map/dot_general | solution.py:17
  67.1 0.8 slice.22
  67.9 2.3 slice.23
  70.2 0.0 all-reduce.3.cloned.1.call-update
  70.2 0.0 all-gather.12.cloned.1.call-start
  70.3 101.9 %all-reduce.3.cloned.1.call-done = (f32[128,1024]{1,0:T(8,128)}, f32[896,1024]{1,0:T(8,128)}) async-done(((f32[128,1024]{1,0:T(8,128)}, f32[896,1024]{1,0:T(8,128)}), (f32[128,1024]{1,0:T(8,128)}, f32[896,1024]{1,0:T(8,128)})) %all-reduce.3.cloned.1.call-update) | async-done | bytes 4194320 | tf_op jit(solution)/shard_map/psum | solution.py:23
  172.2 1.9 broadcast_multiply_fusion.1
  174.1 0.0 all-gather.12.cloned.1.call-update
  174.1 0.0 all-gather.14.cloned.1.call-start
  174.2 46.9 %all-gather.12.cloned.1.call-done = f32[1024,1024]{1,0:T(8,128)} async-done(((f32[128,1024]{1,0:T(8,128)}), f32[1024,1024]{1,0:T(8,128)}) %all-gather.12.cloned.1.call-update) | async-done | bytes 4194320 | tf_op jit(solution)/shard_map/all_gather | solution.py:24
  221.2 17.1 %gather_fusion = f32[1024]{0:T(1024)S(1)} fusion(f32[1024,1024]{1,0:T(8,128)} %all-gather.12.cloned.1.call-done, s32[1024]{0:T(1024)S(1)} %bitcast.16), kind=kCustom, calls=%fused_computation | custom fusion | bytes 16384 | tf_op jit(solution)/shard_map/jit(diagonal)/cond/branch_0_fun/gather | solution.py:26
  238.2 0.6 reduce_sum.18
  239.5 3.9 multiply_reduce_fusion
  244.0 4.7 fusion.16
  248.8 2.5 fusion.28
  251.3 0.0 all-gather.14.cloned.1.call-update
  251.3 0.0 all-gather.16.cloned.1.call-start
  251.3 4.7 fusion.15
  256.0 23.4 %all-gather.14.cloned.1.call-done = bf16[1024,1024]{1,0:T(8,128)(2,1)} async-done(((bf16[128,1024]{1,0:T(8,128)(2,1)}), bf16[1024,1024]{1,0:T(8,128)(2,1)}) %all-gather.14.cloned.1.call-update) | async-done | bytes 2097168 | tf_op jit(solution)/shard_map/all_gather | solution.py:36
  279.4 3.3 fusion.29
  282.7 0.0 all-gather.16.cloned.1.call-update
  282.8 0.2 all-gather.18.cloned.1.call-start
  283.0 4.7 fusion.14
  287.7 23.8 %all-gather.16.cloned.1.call-done = bf16[1024,1024]{1,0:T(8,128)(2,1)} async-done(((bf16[128,1024]{1,0:T(8,128)(2,1)}), bf16[1024,1024]{1,0:T(8,128)(2,1)}) %all-gather.16.cloned.1.call-update) | async-done | bytes 2097168 | tf_op jit(solution)/shard_map/all_gather | solution.py:36
  311.5 3.3 fusion.30
  314.9 0.0 all-gather.18.cloned.1.call-update
  314.9 0.0 all-gather.8.cloned.1.call-start
  314.9 2.3 fusion.17
  317.2 0.0 all-gather.8.cloned.1.call-update
  317.2 0.0 all-gather.20.cloned.1.call-start
  317.3 4.7 fusion.13
  322.0 21.6 %all-gather.18.cloned.1.call-done = bf16[1024,1024]{1,0:T(8,128)(2,1)} async-done(((bf16[128,1024]{1,0:T(8,128)(2,1)}), bf16[1024,1024]{1,0:T(8,128)(2,1)}) %all-gather.18.cloned.1.call-update) | async-done | bytes 2097168 | tf_op jit(solution)/shard_map/all_gather | solution.py:36
  343.6 3.4 convolution_subtract_fusion
  347.0 0.0 all-gather.20.cloned.1.call-update
  347.0 4.6 broadcast_multiply_fusion
  351.6 0.0 copy-start.1
  351.6 40.8 %all-gather.8.cloned.1.call-done = bf16[2048,1024]{1,0:T(8,128)(2,1)} async-done(((bf16[2048,128]{1,0:T(8,128)(2,1)}), bf16[2048,1024]{1,0:T(8,128)(2,1)}) %all-gather.8.cloned.1.call-update) | async-done | bytes 4194320 | tf_op jit(solution)/shard_map/all_gather | solution.py:47
  392.4 46.7 %all-gather.20.cloned.1.call-done = f32[1024,1024]{1,0:T(8,128)} async-done(((f32[128,1024]{1,0:T(8,128)}), f32[1024,1024]{1,0:T(8,128)}) %all-gather.20.cloned.1.call-update) | async-done | bytes 4194320 | tf_op jit(solution)/shard_map/all_gather | solution.py:41
  439.1 16.8 %fusion.32 = f32[2048,1024]{1,0:T(8,128)S(1)} fusion(bf16[2048,1024]{1,0:T(8,128)(2,1)} %all-gather.8.cloned.1.call-done, f32[1024,1024]{1,0:T(8,128)} %all-gather.20.cloned.1.call-done), kind=kOutput, calls=%fused_computation.43 | convolution fusion | flops 25769803776 | bytes 16777216 | tf_op jit(solution)/shard_map/dot_general | solution.py:48
  455.9 0.0 copy-done.1
  455.9 0.0 copy-done
  455.9 0.0 copy-done.2
  455.9 30.5 %multiply_convert_fusion = bf16[2048,1024]{1,0:T(8,128)(2,1)} fusion(bf16[2048,1024]{1,0:T(8,128)(2,1)S(1)} %copy-done.2, s32[2048,1024]{1,0:T(8,128)} %param.5, f32[2048,1024]{1,0:T(8,128)S(1)} %fusion.32, f32[896,1024]{1,0:T(8,128)S(1)} %copy-done, f32[128,1024]{1,0:T(8,128)S(1)} %copy-done.1), kind=kOutput, calls=%fused_computation.1 | convolution fusion | flops 25781338112 | bytes 29360128 | tf_op jit(solution)/shard_map/dot_general | solution.py:49
  (4 shorter events, 0.0 us)
Async XLA Ops:
  6.5 53.0 %all-gather.10.cloned.1.call-start = ((), (), s32[]{:S(2)}) async-start(), calls=%async_computation.1 | async-start | bytes 4718592 | tf_op jit(solution)/shard_map/all_gather | solution.py:19
  8.4 163.8 %all-reduce.3.cloned.1.call-start = ((), (), s32[]{:S(2)}) async-start(), calls=%async_computation.7 | async-start | bytes 8388608 | tf_op jit(solution)/shard_map/psum | solution.py:23
  70.2 150.9 %all-gather.12.cloned.1.call-start = ((), (), s32[]{:S(2)}) async-start(), calls=%async_computation.2 | async-start | bytes 4718592 | tf_op jit(solution)/shard_map/all_gather | solution.py:24
  174.1 105.3 %all-gather.14.cloned.1.call-start = ((), (), s32[]{:S(2)}) async-start(), calls=%async_computation.3 | async-start | bytes 2359296 | tf_op jit(solution)/shard_map/all_gather | solution.py:36
  251.3 60.2 %all-gather.16.cloned.1.call-start = ((), (), s32[]{:S(2)}) async-start(), calls=%async_computation.4 | async-start | bytes 2359296 | tf_op jit(solution)/shard_map/all_gather | solution.py:36
  282.8 60.8 %all-gather.18.cloned.1.call-start = ((), (), s32[]{:S(2)}) async-start(), calls=%async_computation.5 | async-start | bytes 2359296 | tf_op jit(solution)/shard_map/all_gather | solution.py:36
  314.9 77.5 %all-gather.8.cloned.1.call-start = ((), (), s32[]{:S(2)}) async-start(), calls=%async_computation | async-start | bytes 4718592 | tf_op jit(solution)/shard_map/all_gather | solution.py:47
  317.2 121.8 %all-gather.20.cloned.1.call-start = ((), (), s32[]{:S(2)}) async-start(), calls=%async_computation.6 | async-start | bytes 4718592 | tf_op jit(solution)/shard_map/all_gather | solution.py:41
  351.6 104.3 %copy-start.1 = (f32[128,1024]{1,0:T(8,128)S(1)}, f32[128,1024]{1,0:T(8,128)}, u32[]{:S(2)}) copy-start(f32[128,1024]{1,0:T(8,128)} %broadcast_multiply_fusion.1) | copy-start | bytes 1572868
  439.1 16.8 %copy-start = (f32[896,1024]{1,0:T(8,128)S(1)}, f32[896,1024]{1,0:T(8,128)}, u32[]{:S(2)}) copy-start(f32[896,1024]{1,0:T(8,128)} %broadcast_multiply_fusion) | copy-start | bytes 11010052
  439.1 16.8 %copy-start.2 = (bf16[2048,1024]{1,0:T(8,128)(2,1)S(1)}, bf16[2048,1024]{1,0:T(8,128)(2,1)}, u32[]{:S(2)}) copy-start(bf16[2048,1024]{1,0:T(8,128)(2,1)} %param.4) | copy-start | bytes 12582916
Sparse Core Ops, SparseCore 0:
  8.9 50.5 all-gather.9
  70.3 101.8 all-reduce.2
  174.3 46.8 all-gather.11
  251.4 27.9 all-gather.13
  282.9 28.6 all-gather.15
  315.0 28.5 all-gather.17
  345.2 47.2 all-gather.7
  394.0 45.0 all-gather.19
where the time goes:
time: 494 us; the launch traced here: 493 us
  waiting for transfers between devices  356 us (72%)
  matrix products  86.3 us (17%)
  local copies, waits for them, and re-layouts  22.1 us (4%)
  between operations  14.9 us (3%)
  other arithmetic  13.3 us (3%)
    psum x1, waiting for transfers between devices, per_device(): block_part = lax.psum(partial_panel[:panel_width], 'tok') / total_count  102 us
    all_gather x3, waiting for transfers between devices, per_device(): lax.all_gather(iterate.astype(jnp.bfloat16), 'col', axis=0, tiled=True)  68.8 us
    all_gather x1, waiting for transfers between devices, per_device(): lax.all_gather(activations[:, :panel_width], 'col', axis=1, tiled=True)  51 us
    all_gather x1, waiting for transfers between devices, per_device(): diagonal_block = lax.all_gather(block_part, 'col', axis=0, tiled=True)  46.9 us
    all_gather x1, waiting for transfers between devices, per_device(): inverse = lax.all_gather(iterate, 'col', axis=0, tiled=True)  46.7 us
    all_gather x1, waiting for transfers between devices, per_device(): lax.all_gather(pruned, 'col', axis=1, tiled=True).astype(jnp.float32)  40.8 us
    dot_general x1, matrix products, per_device(): lax.dot_general(factor_rows, hessian_panel, (((1,), (1,)), ((), ())), pre...  30.5 us
    dot_general x4, matrix products, per_device(): product = jnp.dot(iterate, damped, precision=highest)  18.8 us
  transfers between devices with their start and end apart: 8, of which 8 were waited for; matrix products, arithmetic and copies ran while one was open for 5% of the time, Pallas kernels for 0%

commit v1 on v0

--- a/solution.py
+++ b/solution.py
@@ -21,7 +21,12 @@
         preferred_element_type=jnp.float32,
     )
     block_part = lax.psum(partial_panel[:panel_width], "tok") / total_count
-    diagonal_block = lax.all_gather(block_part, "col", axis=0, tiled=True)
+    ring = [block_part]
+    for hop in range(7):
+        ring.append(lax.ppermute(ring[-1], "col", [(dev, (dev + 1) % 8) for dev in range(8)]))
+    diagonal_block = jnp.roll(
+        jnp.concatenate(ring[::-1], axis=0), (lax.axis_index("col") + 1) * ring[0].shape[0], axis=0
+    )
     identity = jnp.eye(B, dtype=jnp.float32)
     damping = 0.01 * jnp.mean(jnp.diagonal(diagonal_block))
     damped = diagonal_block + damping * identity

time: 494 us -> 528 us (1.069)
  waiting for transfers between devices: 356 us -> 380 us
  local copies, waits for them, and re-layouts: 22.1 us -> 31.5 us
    ppermute x0 -> x7, waiting for transfers between devices: none -> 73.2 us  [per_device(): lax.ppermute(ring[-1], 'col', [(dev, (dev + 1) % 8) for dev in range(8)])]
    all_gather x1 -> x0, waiting for transfers between devices: 46.9 us -> none  [per_device(): diagonal_block = lax.all_gather(block_part, 'col', axis=0, tiled=True)]
    unnamed x6 -> x26, local copies, waits for them, and re-layouts: 0.01 us -> 6.7 us
  transfers between devices with their start and end apart: 8 -> 14, of which waited for: 8 -> 14; matrix products, arithmetic and copies ran while one was open for 5% -> 5% of each run, Pallas kernels for 0% -> 0%
where the time goes in v1:
time: 528 us; the launch traced here: 527 us
  waiting for transfers between devices  380 us (72%)
  matrix products  86.3 us (16%)
  local copies, waits for them, and re-layouts  31.5 us (6%)
  between operations  15 us (3%)
  other arithmetic  12.8 us (2%)
    psum x1, waiting for transfers between devices, per_device(): block_part = lax.psum(partial_panel[:panel_width], 'tok') / total_count  102 us
    ppermute x7, waiting for transfers between devices, per_device(): lax.ppermute(ring[-1], 'col', [(dev, (dev + 1) % 8) for dev in range(8)])  73.2 us
    all_gather x3, waiting for transfers between devices, per_device(): lax.all_gather(iterate.astype(jnp.bfloat16), 'col', axis=0, tiled=True)  66.8 us
    all_gather x1, waiting for transfers between devices, per_device(): lax.all_gather(activations[:, :panel_width], 'col', axis=1, tiled=True)  51 us
    all_gather x1, waiting for transfers between devices, per_device(): inverse = lax.all_gather(iterate, 'col', axis=0, tiled=True)  46.7 us
    all_gather x1, waiting for transfers between devices, per_device(): lax.all_gather(pruned, 'col', axis=1, tiled=True).astype(jnp.float32)  40.7 us
    dot_general x1, matrix products, per_device(): lax.dot_general(factor_rows, hessian_panel, (((1,), (1,)), ((), ())), pre...  30.6 us
    dot_general x4, matrix products, per_device(): product = jnp.dot(iterate, damped, precision=highest)  18.8 us
  transfers between devices with their start and end apart: 14, of which 14 were waited for; matrix products, arithmetic and copies ran while one was open for 5% of the time, Pallas kernels for 0%

profile of v1, /device:TPU:0, one launch (start us, length us, event | category | flops | bytes accessed | tf_op | source)
XLA Modules:
  0.0 526.8 jit_solution(8335016707694100384)
XLA Ops:
  6.5 1.9 slice.17
  8.4 0.0 all-gather.9.cloned.1.call-update
  8.4 0.0 all-reduce.3.cloned.1.call-start
  8.5 51.0 %all-gather.9.cloned.1.call-done = bf16[2048,1024]{1,0:T(8,128)(2,1)} async-done(((bf16[2048,128]{1,0:T(8,128)(2,1)}), bf16[2048,1024]{1,0:T(8,128)(2,1)}) %all-gather.9.cloned.1.call-update) | async-done | bytes 4194320 | tf_op jit(solution)/shard_map/all_gather | solution.py:19
  59.5 7.6 %fusion.31 = f32[1024,1024]{1,0:T(8,128)S(1)} fusion(bf16[2048,1024]{1,0:T(8,128)(2,1)} %param.3, bf16[2048,1024]{1,0:T(8,128)(2,1)} %all-gather.9.cloned.1.call-done), kind=kOutput, calls=%fused_computation.59 | convolution fusion | flops 4294967296 | bytes 12582912 | tf_op jit(solution)/shard_map/dot_general | solution.py:17
  67.1 2.3 slice.23
  69.4 0.8 slice.22
  70.2 0.0 all-gather.11.cloned.1.call-start
  70.3 101.9 %all-reduce.3.cloned.1.call-done = (f32[128,1024]{1,0:T(8,128)}, f32[896,1024]{1,0:T(8,128)}) async-done(((f32[128,1024]{1,0:T(8,128)}, f32[896,1024]{1,0:T(8,128)}), (f32[128,1024]{1,0:T(8,128)}, f32[896,1024]{1,0:T(8,128)})) %all-reduce.3.cloned.1.call-update) | async-done | bytes 4194320 | tf_op jit(solution)/shard_map/psum | solution.py:23
  172.2 1.1 broadcast_multiply_fusion.1
  173.4 0.1 collective-permute-start
  173.4 10.4 %collective-permute-done = f32[128,1024]{1,0:T(8,128)S(1)} collective-permute-done((f32[128,1024]{1,0:T(8,128)S(1)}, f32[128,1024]{1,0:T(8,128)S(1)}, u32[]{:S(2)}, u32[]{:S(2)}) %collective-permute-start) | collective-permute-done | bytes 524320 | tf_op jit(solution)/shard_map/ppermute | solution.py:26
  183.8 10.4 %collective-permute-done.1 = f32[128,1024]{1,0:T(8,128)S(1)} collective-permute-done((f32[128,1024]{1,0:T(8,128)S(1)}, f32[128,1024]{1,0:T(8,128)S(1)}, u32[]{:S(2)}, u32[]{:S(2)}) %collective-permute-start.1) | collective-permute-done | bytes 524320 | tf_op jit(solution)/shard_map/ppermute | solution.py:26
  194.2 10.4 %collective-permute-done.2 = f32[128,1024]{1,0:T(8,128)S(1)} collective-permute-done((f32[128,1024]{1,0:T(8,128)S(1)}, f32[128,1024]{1,0:T(8,128)S(1)}, u32[]{:S(2)}, u32[]{:S(2)}) %collective-permute-start.2) | collective-permute-done | bytes 524320 | tf_op jit(solution)/shard_map/ppermute | solution.py:26
  204.6 10.4 %collective-permute-done.3 = f32[128,1024]{1,0:T(8,128)S(1)} collective-permute-done((f32[128,1024]{1,0:T(8,128)S(1)}, f32[128,1024]{1,0:T(8,128)S(1)}, u32[]{:S(2)}, u32[]{:S(2)}) %collective-permute-start.3) | collective-permute-done | bytes 524320 | tf_op jit(solution)/shard_map/ppermute | solution.py:26
  215.0 10.4 %collective-permute-done.4 = f32[128,1024]{1,0:T(8,128)S(1)} collective-permute-done((f32[128,1024]{1,0:T(8,128)S(1)}, f32[128,1024]{1,0:T(8,128)S(1)}, u32[]{:S(2)}, u32[]{:S(2)}) %collective-permute-start.4) | collective-permute-done | bytes 524320 | tf_op jit(solution)/shard_map/ppermute | solution.py:26
  225.4 10.5 %collective-permute-done.5 = f32[128,1024]{1,0:T(8,128)} collective-permute-done((f32[128,1024]{1,0:T(8,128)S(1)}, f32[128,1024]{1,0:T(8,128)}, u32[]{:S(2)}, u32[]{:S(2)}) %collective-permute-start.5) | collective-permute-done | bytes 524320 | tf_op jit(solution)/shard_map/ppermute | solution.py:26
  236.0 10.7 %collective-permute-done.6 = f32[128,1024]{1,0:T(8,128)} collective-permute-done((f32[128,1024]{1,0:T(8,128)}, f32[128,1024]{1,0:T(8,128)}, u32[]{:S(2)}, u32[]{:S(2)}) %collective-permute-start.6) | collective-permute-done | bytes 524320 | tf_op jit(solution)/shard_map/ppermute | solution.py:26
  246.7 1.1 constant_dynamic-update-slice_fusion.15
  247.8 1.1 constant_dynamic-update-slice_fusion.14
  249.1 1.1 constant_dynamic-update-slice_fusion.7
  250.2 1.1 constant_dynamic-update-slice_fusion.6
  251.6 2.5 constant_dynamic-slice_fusion
  254.1 2.0 copy-done
  256.1 17.2 %gather_fusion = f32[1024]{0:T(1024)S(1)} fusion(f32[1024,1024]{1,0:T(8,128)} %constant_dynamic-slice_fusion, s32[1024]{0:T(1024)S(1)} %bitcast.16), kind=kCustom, calls=%fused_computation | custom fusion | bytes 16384 | tf_op jit(solution)/shard_map/jit(diagonal)/cond/branch_0_fun/gather | solution.py:31
  273.4 0.7 reduce_sum.18
  274.6 3.9 multiply_reduce_fusion
  279.2 4.7 fusion.16
  283.9 2.5 fusion.28
  286.5 0.2 all-gather.13.cloned.1.call-start
  286.7 4.7 fusion.15
  291.4 21.6 %all-gather.11.cloned.1.call-done = bf16[1024,1024]{1,0:T(8,128)(2,1)} async-done(((bf16[128,1024]{1,0:T(8,128)(2,1)}), bf16[1024,1024]{1,0:T(8,128)(2,1)}) %all-gather.11.cloned.1.call-update) | async-done | bytes 2097168 | tf_op jit(solution)/shard_map/all_gather | solution.py:41
  313.0 3.3 fusion.29
  316.4 0.0 all-gather.15.cloned.1.call-start
  316.4 4.7 fusion.14
  321.1 24.0 %all-gather.13.cloned.1.call-done = bf16[1024,1024]{1,0:T(8,128)(2,1)} async-done(((bf16[128,1024]{1,0:T(8,128)(2,1)}), bf16[1024,1024]{1,0:T(8,128)(2,1)}) %all-gather.13.cloned.1.call-update) | async-done | bytes 2097168 | tf_op jit(solution)/shard_map/all_gather | solution.py:41
  345.1 3.3 fusion.30
  348.4 0.0 all-gather.7.cloned.1.call-start
  348.5 2.4 fusion.17
  350.9 0.3 all-gather.17.cloned.1.call-start
  351.1 4.7 fusion.13
  355.8 21.3 %all-gather.15.cloned.1.call-done = bf16[1024,1024]{1,0:T(8,128)(2,1)} async-done(((bf16[128,1024]{1,0:T(8,128)(2,1)}), bf16[1024,1024]{1,0:T(8,128)(2,1)}) %all-gather.15.cloned.1.call-update) | async-done | bytes 2097168 | tf_op jit(solution)/shard_map/all_gather | solution.py:41
  377.1 3.4 convolution_subtract_fusion
  380.6 4.6 broadcast_multiply_fusion
  385.1 40.7 %all-gather.7.cloned.1.call-done = bf16[2048,1024]{1,0:T(8,128)(2,1)} async-done(((bf16[2048,128]{1,0:T(8,128)(2,1)}), bf16[2048,1024]{1,0:T(8,128)(2,1)}) %all-gather.7.cloned.1.call-update) | async-done | bytes 4194320 | tf_op jit(solution)/shard_map/all_gather | solution.py:52
  425.8 46.7 %all-gather.17.cloned.1.call-done = f32[1024,1024]{1,0:T(8,128)} async-done(((f32[128,1024]{1,0:T(8,128)}), f32[1024,1024]{1,0:T(8,128)}) %all-gather.17.cloned.1.call-update) | async-done | bytes 4194320 | tf_op jit(solution)/shard_map/all_gather | solution.py:46
  472.5 16.8 %fusion.32 = f32[2048,1024]{1,0:T(8,128)S(1)} fusion(bf16[2048,1024]{1,0:T(8,128)(2,1)} %all-gather.7.cloned.1.call-done, f32[1024,1024]{1,0:T(8,128)} %all-gather.17.cloned.1.call-done), kind=kOutput, calls=%fused_computation.60 | convolution fusion | flops 25769803776 | bytes 16777216 | tf_op jit(solution)/shard_map/dot_general | solution.py:53
  489.3 30.6 %multiply_convert_fusion = bf16[2048,1024]{1,0:T(8,128)(2,1)} fusion(bf16[2048,1024]{1,0:T(8,128)(2,1)S(1)} %copy-done.5, s32[2048,1024]{1,0:T(8,128)} %param.5, f32[2048,1024]{1,0:T(8,128)S(1)} %fusion.32, f32[896,1024]{1,0:T(8,128)S(1)} %copy-done.2, f32[128,1024]{1,0:T(8,128)S(1)} %copy-done.4), kind=kOutput, calls=%fused_computation.1 | convolution fusion | flops 25781338112 | bytes 29360128 | tf_op jit(solution)/shard_map/dot_general | solution.py:54
  (38 shorter events, 0.6 us)
Async XLA Ops:
  6.5 53.0 %all-gather.9.cloned.1.call-start = ((), (), s32[]{:S(2)}) async-start(), calls=%async_computation.1 | async-start | bytes 4718592 | tf_op jit(solution)/shard_map/all_gather | solution.py:19
  8.4 163.8 %all-reduce.3.cloned.1.call-start = ((), (), s32[]{:S(2)}) async-start(), calls=%async_computation.6 | async-start | bytes 8388608 | tf_op jit(solution)/shard_map/psum | solution.py:23
  70.2 242.8 %all-gather.11.cloned.1.call-start = ((), (), s32[]{:S(2)}) async-start(), calls=%async_computation.2 | async-start | bytes 2359296 | tf_op jit(solution)/shard_map/all_gather | solution.py:41
  172.2 76.9 %copy-start.1 = (f32[128,1024]{1,0:T(8,128)S(1)}, f32[128,1024]{1,0:T(8,128)}, u32[]{:S(2)}) copy-start(f32[128,1024]{1,0:T(8,128)} %get-tuple-element.5) | copy-start | bytes 1572868
  173.4 62.6 %copy-start.3 = (f32[128,1024]{1,0:T(8,128)}, f32[128,1024]{1,0:T(8,128)S(1)}, u32[]{:S(2)}) copy-start(f32[128,1024]{1,0:T(8,128)S(1)} %broadcast_multiply_fusion.1) | copy-start | bytes 1572868
  173.4 10.5 %collective-permute-start = (f32[128,1024]{1,0:T(8,128)S(1)}, f32[128,1024]{1,0:T(8,128)S(1)}, u32[]{:S(2)}, u32[]{:S(2)}) collective-permute-start(f32[128,1024]{1,0:T(8,128)S(1)} %broadcast_multiply_fusion.1), channel_id=1, source_target_pairs={{0,1},{1,2},{2,3},{3,4},{4,5},{5,6},{6,7},{7,0},{8,9},{9,10},{10,1... | collective-permute-start | bytes 1572872 | tf_op jit(solution)/shard_map/ppermute | solution.py:26
  183.8 10.4 %collective-permute-start.1 = (f32[128,1024]{1,0:T(8,128)S(1)}, f32[128,1024]{1,0:T(8,128)S(1)}, u32[]{:S(2)}, u32[]{:S(2)}) collective-permute-start(f32[128,1024]{1,0:T(8,128)S(1)} %collective-permute-done), channel_id=1, source_target_pairs={{0,1},{1,2},{2,3},{3,4},{4,5},{5,6},{6,7},{7,0},{8,9},{9,10},{10,1... | collective-permute-start | bytes 1572872 | tf_op jit(solution)/shard_map/ppermute | solution.py:26
  194.2 10.4 %collective-permute-start.2 = (f32[128,1024]{1,0:T(8,128)S(1)}, f32[128,1024]{1,0:T(8,128)S(1)}, u32[]{:S(2)}, u32[]{:S(2)}) collective-permute-start(f32[128,1024]{1,0:T(8,128)S(1)} %collective-permute-done.1), channel_id=1, source_target_pairs={{0,1},{1,2},{2,3},{3,4},{4,5},{5,6},{6,7},{7,0},{8,9},{9,10},{10,1... | collective-permute-start | bytes 1572872 | tf_op jit(solution)/shard_map/ppermute | solution.py:26
  204.6 10.4 %collective-permute-start.3 = (f32[128,1024]{1,0:T(8,128)S(1)}, f32[128,1024]{1,0:T(8,128)S(1)}, u32[]{:S(2)}, u32[]{:S(2)}) collective-permute-start(f32[128,1024]{1,0:T(8,128)S(1)} %collective-permute-done.2), channel_id=1, source_target_pairs={{0,1},{1,2},{2,3},{3,4},{4,5},{5,6},{6,7},{7,0},{8,9},{9,10},{10,1... | collective-permute-start | bytes 1572872 | tf_op jit(solution)/shard_map/ppermute | solution.py:26
  215.0 10.4 %collective-permute-start.4 = (f32[128,1024]{1,0:T(8,128)S(1)}, f32[128,1024]{1,0:T(8,128)S(1)}, u32[]{:S(2)}, u32[]{:S(2)}) collective-permute-start(f32[128,1024]{1,0:T(8,128)S(1)} %collective-permute-done.3), channel_id=1, source_target_pairs={{0,1},{1,2},{2,3},{3,4},{4,5},{5,6},{6,7},{7,0},{8,9},{9,10},{10,1... | collective-permute-start | bytes 1572872 | tf_op jit(solution)/shard_map/ppermute | solution.py:26
  225.4 10.5 %collective-permute-start.5 = (f32[128,1024]{1,0:T(8,128)S(1)}, f32[128,1024]{1,0:T(8,128)}, u32[]{:S(2)}, u32[]{:S(2)}) collective-permute-start(f32[128,1024]{1,0:T(8,128)S(1)} %collective-permute-done.4), channel_id=1, source_target_pairs={{0,1},{1,2},{2,3},{3,4},{4,5},{5,6},{6,7},{7,0},{8,9},{9,10},{10,1... | collective-permute-start | bytes 1572872 | tf_op jit(solution)/shard_map/ppermute | solution.py:26
  236.0 10.7 %collective-permute-start.6 = (f32[128,1024]{1,0:T(8,128)}, f32[128,1024]{1,0:T(8,128)}, u32[]{:S(2)}, u32[]{:S(2)}) collective-permute-start(f32[128,1024]{1,0:T(8,128)} %collective-permute-done.5), channel_id=1, source_target_pairs={{0,1},{1,2},{2,3},{3,4},{4,5},{5,6},{6,7},{7,0},{8,9},{9,10},{10,1... | collective-permute-start | bytes 1572872 | tf_op jit(solution)/shard_map/ppermute | solution.py:26
  251.6 4.5 copy-start
  286.5 58.6 %all-gather.13.cloned.1.call-start = ((), (), s32[]{:S(2)}) async-start(), calls=%async_computation.3 | async-start | bytes 2359296 | tf_op jit(solution)/shard_map/all_gather | solution.py:41
  316.4 60.8 %all-gather.15.cloned.1.call-start = ((), (), s32[]{:S(2)}) async-start(), calls=%async_computation.4 | async-start | bytes 2359296 | tf_op jit(solution)/shard_map/all_gather | solution.py:41
  348.4 77.4 %all-gather.7.cloned.1.call-start = ((), (), s32[]{:S(2)}) async-start(), calls=%async_computation | async-start | bytes 4718592 | tf_op jit(solution)/shard_map/all_gather | solution.py:52
  350.9 121.6 %all-gather.17.cloned.1.call-start = ((), (), s32[]{:S(2)}) async-start(), calls=%async_computation.5 | async-start | bytes 4718592 | tf_op jit(solution)/shard_map/all_gather | solution.py:46
  385.1 104.2 %copy-start.4 = (f32[128,1024]{1,0:T(8,128)S(1)}, f32[128,1024]{1,0:T(8,128)}, u32[]{:S(2)}) copy-start(f32[128,1024]{1,0:T(8,128)} %copy-done.3) | copy-start | bytes 1572868
  472.5 16.8 %copy-start.2 = (f32[896,1024]{1,0:T(8,128)S(1)}, f32[896,1024]{1,0:T(8,128)}, u32[]{:S(2)}) copy-start(f32[896,1024]{1,0:T(8,128)} %broadcast_multiply_fusion) | copy-start | bytes 11010052
  472.5 16.8 %copy-start.5 = (bf16[2048,1024]{1,0:T(8,128)(2,1)S(1)}, bf16[2048,1024]{1,0:T(8,128)(2,1)}, u32[]{:S(2)}) copy-start(bf16[2048,1024]{1,0:T(8,128)(2,1)} %param.4) | copy-start | bytes 12582916
Sparse Core Ops, SparseCore 0:
  8.9 50.5 all-gather.8
  70.3 101.8 all-reduce.2
  286.6 26.3 all-gather.10
  316.5 28.5 all-gather.12
  348.5 28.5 all-gather.14
  378.6 47.2 all-gather.6
  427.4 45.0 all-gather.16
